TPU v7x, 128 devices: a whole 4x4x4 slice. The times are simulated.
128 devices in a mesh: lat: 16 (over z, x_lo, core), vec: 8 (over x_hi, y).
Axes of the slice: x: 4 (x_hi: 2, x_lo: 2; x = x_hi * 2 + x_lo), y: 4, z: 4, core: 2. Of those that a mesh axis runs over, the one named last changes fastest.
Arguments:
- vectors: bfloat16 [4, 128, 256, 1024], P(None, 'vec', 'lat'), may hold values from -6 to 6
- classical_spins: float32 [3, 256, 1024], P(None, 'lat'), may hold values from -1 to 1, as said below
- coefficients: float32 [5], replicated, may hold values from 0.4 to 1.6
Outputs:
- rotated_spins: float32 [3, 256, 1024], P(None, 'lat')
- local_fields: float32 [3, 256, 1024], P(None, 'lat')
Inputs may be any that keep to these rules, and one draw needn't show every extreme that they name: `classical_spins`: each site's spin has unit length.
All inputs are finite; a program needn't handle non-finite values.
Results may differ from a plain program's by a relative error of at most 0.0003.
Values sent between devices are 32-bit elements; how exact they have to be, the bound alone decides.
A program may use at most 64 MiB of HBM per device.

v0:
```python
import jax
import jax.numpy as jnp
from jax import lax
from jax.sharding import PartitionSpec as P

STEPS = 4


coupling = 2.0
hopping = 1.0
inverse_bound = 1.0 / 6.5
time_step = 1.0


def with_halo(block, sides, width):
    for axis, dim in sides:
        count = lax.axis_size(axis)
        forward = [(i, i + 1) for i in range(count - 1)]
        forward.append((count - 1, 0))
        backward = [(target, source) for source, target in forward]
        low = lax.ppermute(
            lax.slice_in_dim(block, block.shape[dim] - width, None, axis=dim), axis, forward
        )
        high = lax.ppermute(lax.slice_in_dim(block, 0, width, axis=dim), axis, backward)
        block = jnp.concatenate([low, block, high], axis=dim)
    return block


def exchange_term(states, spins_here):
    spin_x = spins_here[0][None]
    spin_y = spins_here[1][None]
    spin_z = spins_here[2][None]
    up_real, up_imag, down_real, down_imag = (states[0], states[1], states[2], states[3])
    return jnp.stack(
        [
            spin_z * up_real + spin_x * down_real + spin_y * down_imag,
            spin_z * up_imag + spin_x * down_imag - spin_y * down_real,
            spin_x * up_real - spin_y * up_imag - spin_z * down_real,
            spin_x * up_imag + spin_y * up_real - spin_z * down_imag,
        ]
    )


def spin_density(probes, weighted):
    along_x = jnp.sum(
        probes[0] * weighted[2]
        + probes[1] * weighted[3]
        + probes[2] * weighted[0]
        + probes[3] * weighted[1],
        axis=0,
    )
    along_y = jnp.sum(
        probes[0] * weighted[3]
        - probes[1] * weighted[2]
        - probes[2] * weighted[1]
        + probes[3] * weighted[0],
        axis=0,
    )
    along_z = jnp.sum(
        probes[0] * weighted[0]
        + probes[1] * weighted[1]
        - probes[2] * weighted[2]
        - probes[3] * weighted[3],
        axis=0,
    )
    return jnp.stack([along_x, along_y, along_z])


def rotate_spins(spins_now, fields):
    magnitude = jnp.sqrt(jnp.sum(fields * fields, axis=0))
    rotation_angle = time_step * magnitude
    cosine = jnp.cos(rotation_angle)
    sine_ratio = jnp.sinc(rotation_angle / jnp.pi)
    half_ratio = 0.5 * jnp.sinc(rotation_angle / (2.0 * jnp.pi)) ** 2
    torque = jnp.cross(fields, spins_now, axis=0)
    projection = jnp.sum(fields * spins_now, axis=0)
    return (
        cosine * spins_now
        + time_step * sine_ratio * torque
        + time_step * time_step * half_ratio * projection * fields
    )


def apply_hamiltonian(padded, spins_here):
    middle = padded[:, :, 1:-1]
    neighbours = (
        padded[:, :, 2:] + padded[:, :, :-2] + jnp.roll(middle, 1, 3) + jnp.roll(middle, -1, 3)
    )
    return inverse_bound * (coupling * exchange_term(middle, spins_here) - hopping * neighbours)


def shards(vectors, classical_spins, coefficients):
    probes = vectors.astype(jnp.float32)
    count_all = vectors.shape[1] * lax.axis_size("vec")
    moments = coefficients[0] * probes
    previous = probes
    current = probes
    for degree in range(STEPS):
        padded = with_halo(current, (("lat", 2),), 1)
        following = apply_hamiltonian(padded, classical_spins)
        if degree > 0:
            following = 2.0 * following - previous
        moments = moments + coefficients[degree + 1] * following
        previous = current
        current = following
    partial_value = spin_density(probes, moments) * (coupling / count_all)
    fields = lax.psum(partial_value, "vec")
    rotated = rotate_spins(classical_spins, fields)
    return (rotated, fields)


def solution(mesh):
    placed = (P(None, "vec", "lat", None), P(None, "lat", None), P())
    return jax.shard_map(
        shards,
        mesh=mesh,
        in_specs=placed,
        out_specs=(P(None, "lat", None), P(None, "lat", None)),
        check_vma=False,
    )
```

profile of v0, /device:TPU:0, one launch (start us, length us, event | category | flops | bytes accessed | tf_op | source)
XLA Modules:
  0.0 194.6 jit_solution(3503848978186060714)
XLA Ops:
  7.2 0.0 all-reduce.2.cloned.1.call-start
  7.2 2.8 %copy_convert_fusion = f32[4,16,16,1024]{3,1,2,0:T(8,128)S(1)} fusion(bf16[4,16,16,1024]{3,2,1,0:T(8,128)(2,1)} %param.4), kind=kLoop, calls=%fused_computation.36 | loop fusion | flops 1048576 | bytes 6291456 | tf_op jit(solution)/shard_map/convert_element_type | solution.py:93
  10.1 0.1 collective-permute-start.1
  10.2 0.0 copy-start.2
  10.2 0.0 copy-start.3
  10.2 4.6 %collective-permute-start = (f32[4,16,1,1024]{3,1,2,0:T(8,128)S(1)}, f32[4,16,1,1024]{3,1,2,0:T(8,128)S(1)}, u32[]{:S(2)}, u32[]{:S(2)}) collective-permute-start(f32[4,16,1,1024]{3,1,2,0:T(8,128)S(1)} %get-tuple-element.44), channel_id=1, source_target_pairs={{8,0},{16,8},{24,16},{32,24},{40,32},{48,40},{56,48},{64,56},{72,6... | collective-permute-start | bytes 786440 | tf_op jit(solution)/shard_map/ppermute | solution.py:24
  14.8 1.7 fusion.65
  16.5 0.0 copy-done.2
  16.5 0.0 copy-done.3
  16.5 0.6 fusion.66
  17.7 0.9 multiply_add_fusion.3
  18.6 0.2 fusion.64
  18.8 0.1 collective-permute-done.1
  18.9 0.0 collective-permute-done
  19.0 4.2 %broadcast_multiply_fusion = (f32[4,16,16,1024]{3,1,2,0:T(8,128)S(1)}, f32[4,16,16,1024]{3,1,2,0:T(8,128)}) fusion(f32[4,16,16,1]{3,1,2,0:T(8,128)S(1)} %get-tuple-element.47, f32[4,16,16,1023]{3,1,2,0:T(8,128)S(1)} %get-tuple-element.49, f32[4,16,16,1023]{3,1,2,0:T(8,128)S(1)} %get-tuple-element.48, f32[4,16,16,1]{3,1,2,0:T(8,128)S(1)} %get-tuple-element.46, ...), kind=kLoop, calls=%fused_computation.37 | loop fusion | flops 13631488 | bytes 25690112 | tf_op jit(solution)/shard_map/mul | solution.py:89
  23.2 2.1 %multiply_add_fusion.2 = (f32[1,16,16,1024]{3,1,2,0:T(8,128)S(1)}, f32[1,16,16,1024]{3,1,2,0:T(8,128)S(1)}, f32[1,16,16,1024]{3,1,2,0:T(8,128)}, f32[1,16,16,1024]{3,1,2,0:T(8,128)}) fusion(f32[4,16,16,1024]{3,1,2,0:T(8,128)S(1)} %get-tuple-element.7, f32[16,1024]{1,0:T(8,128)S(1)} %get-tuple-element.54, f32[16,1024]{1,0:T(8,128)S(1)} %get-tuple-element.55, ...), kind=kLoop, calls=%fused_computation.52 | loop fusion | flops 5242880 | bytes 8585216 | tf_op jit(solution)/shard_map/add | solution.py:36
  25.3 0.0 copy-start.1
  25.3 3.4 %fusion.60 = (f32[4,16,16,1023]{3,1,2,0:T(8,128)S(1)}, f32[4,16,16,1023]{3,1,2,0:T(8,128)}) fusion(f32[4,16,16,1024]{3,1,2,0:T(8,128)S(1)} %get-tuple-element.7), kind=kLoop, calls=%fused_computation.125 | loop fusion | bytes 16760832 | tf_op jit(solution)/shard_map/jit(_roll_static)/slice | solution.py:87
  28.7 1.1 collective-permute-start.3
  29.8 2.7 %collective-permute-start.2 = (f32[4,16,1,1024]{3,1,2,0:T(8,128)S(1)}, f32[4,16,1,1024]{3,1,2,0:T(8,128)S(1)}, u32[]{:S(2)}, u32[]{:S(2)}) collective-permute-start(f32[4,16,1,1024]{3,1,2,0:T(8,128)S(1)} %get-tuple-element.42), channel_id=1, source_target_pairs={{8,0},{16,8},{24,16},{32,24},{40,32},{48,40},{56,48},{64,56},{72,6... | collective-permute-start | bytes 786440 | tf_op jit(solution)/shard_map/ppermute | solution.py:24
  32.6 0.2 fusion.61
  32.8 5.3 %collective-permute-done.3 = f32[4,16,1,1024]{3,1,2,0:T(8,128)S(1)} collective-permute-done((f32[4,16,1,1024]{3,1,2,0:T(8,128)S(1)}, f32[4,16,1,1024]{3,1,2,0:T(8,128)S(1)}, u32[]{:S(2)}, u32[]{:S(2)}) %collective-permute-start.3) | collective-permute-done | bytes 262176 | tf_op jit(solution)/shard_map/ppermute | solution.py:21
  38.1 0.0 collective-permute-done.2
  38.1 0.0 copy-done.1
  38.1 5.5 %fusion.19 = f32[4,16,16,1024]{3,1,2,0:T(8,128)S(1)} fusion(f32[4,16,16,1024]{3,1,2,0:T(8,128)S(1)} %get-tuple-element.7, f32[4,16,1,1024]{3,1,2,0:T(8,128)S(1)} %collective-permute-done.3, f32[4,16,1,1024]{3,1,2,0:T(8,128)S(1)} %collective-permute-done.2, f32[1,16,16,1024]{3,1,2,0:T(8,128)} %get-tuple-element.21, f32[1,16,16,1024]{3,1,2,0:T(8,128)} %get-tuple-element.20, ...), kind=kLoop, calls=%fused_computation.24 | loop fusion | flops 15728640 | bytes 23592960 | tf_op jit(solution)/shard_map/sub | solution.py:102
  43.6 0.7 multiply_add_fusion.1
  44.4 0.0 copy-start
  44.4 4.7 %fusion.57 = (f32[4,16,16,1023]{3,1,2,0:T(8,128)}, f32[4,16,16,1023]{3,1,2,0:T(8,128)}) fusion(f32[4,16,16,1024]{3,1,2,0:T(8,128)S(1)} %fusion.19), kind=kLoop, calls=%fused_computation.122 | loop fusion | bytes 16760832 | tf_op jit(solution)/shard_map/jit(_roll_static)/slice | solution.py:87
  49.0 0.1 collective-permute-start.5
  49.1 3.7 %collective-permute-start.4 = (f32[4,16,1,1024]{3,1,2,0:T(8,128)S(1)}, f32[4,16,1,1024]{3,1,2,0:T(8,128)S(1)}, u32[]{:S(2)}, u32[]{:S(2)}) collective-permute-start(f32[4,16,1,1024]{3,1,2,0:T(8,128)S(1)} %get-tuple-element.36), channel_id=1, source_target_pairs={{8,0},{16,8},{24,16},{32,24},{40,32},{48,40},{56,48},{64,56},{72,6... | collective-permute-start | bytes 786440 | tf_op jit(solution)/shard_map/ppermute | solution.py:24
  52.9 0.2 fusion.58
  53.1 6.2 %collective-permute-done.5 = f32[4,16,1,1024]{3,1,2,0:T(8,128)S(1)} collective-permute-done((f32[4,16,1,1024]{3,1,2,0:T(8,128)S(1)}, f32[4,16,1,1024]{3,1,2,0:T(8,128)S(1)}, u32[]{:S(2)}, u32[]{:S(2)}) %collective-permute-start.5) | collective-permute-done | bytes 262176 | tf_op jit(solution)/shard_map/ppermute | solution.py:21
  59.3 0.0 collective-permute-done.4
  59.3 0.0 copy-done
  59.3 5.4 %fusion.13 = f32[4,16,16,1024]{3,1,2,0:T(8,128)S(1)} fusion(f32[4,16,16,1024]{3,1,2,0:T(8,128)S(1)} %fusion.19, f32[4,16,1,1024]{3,1,2,0:T(8,128)S(1)} %collective-permute-done.5, f32[4,16,1,1024]{3,1,2,0:T(8,128)S(1)} %collective-permute-done.4, f32[1,16,16,1024]{3,1,2,0:T(8,128)S(1)} %get-tuple-element.17, f32[1,16,16,1024]{3,1,2,0:T(8,128)S(1)} %get-tuple-element.16, ...), kind=kLoop, calls=%fused_computation.16 | loop fusion | flops 15728640 | bytes 25690112 | tf_op jit(solution)/shard_map/sub | solution.py:102
  64.7 2.4 %multiply_add_fusion = (f32[1,16,16,1024]{3,1,2,0:T(8,128)S(1)}, f32[1,16,16,1024]{3,1,2,0:T(8,128)}, f32[1,16,16,1024]{3,1,2,0:T(8,128)}, f32[1,16,16,1024]{3,1,2,0:T(8,128)}) fusion(f32[4,16,16,1024]{3,1,2,0:T(8,128)S(1)} %fusion.13, f32[16,1024]{1,0:T(8,128)S(1)} %get-tuple-element.54, f32[16,1024]{1,0:T(8,128)S(1)} %get-tuple-element.55, ...), kind=kLoop, calls=%fused_computation.44 | loop fusion | flops 5242880 | bytes 8585216 | tf_op jit(solution)/shard_map/add | solution.py:36
  67.1 4.7 %fusion.54 = (f32[4,16,16,1023]{3,1,2,0:T(8,128)}, f32[4,16,16,1023]{3,1,2,0:T(8,128)}) fusion(f32[4,16,16,1024]{3,1,2,0:T(8,128)S(1)} %fusion.13), kind=kLoop, calls=%fused_computation.119 | loop fusion | bytes 16760832 | tf_op jit(solution)/shard_map/jit(_roll_static)/slice | solution.py:87
  71.8 0.0 collective-permute-start.7
  71.8 3.9 %collective-permute-start.6 = (f32[4,16,1,1024]{3,1,2,0:T(8,128)S(1)}, f32[4,16,1,1024]{3,1,2,0:T(8,128)}, u32[]{:S(2)}, u32[]{:S(2)}) collective-permute-start(f32[4,16,1,1024]{3,1,2,0:T(8,128)S(1)} %get-tuple-element.30), channel_id=1, source_target_pairs={{8,0},{16,8},{24,16},{32,24},{40,32},{48,40},{56,48},{64,56},{72,6... | collective-permute-start | bytes 786440 | tf_op jit(solution)/shard_map/ppermute | solution.py:24
  75.6 1.0 fusion.55
  76.7 4.2 %collective-permute-done.7 = f32[4,16,1,1024]{3,1,2,0:T(8,128)S(1)} collective-permute-done((f32[4,16,1,1024]{3,1,2,0:T(8,128)S(1)}, f32[4,16,1,1024]{3,1,2,0:T(8,128)S(1)}, u32[]{:S(2)}, u32[]{:S(2)}) %collective-permute-start.7) | collective-permute-done | bytes 262176 | tf_op jit(solution)/shard_map/ppermute | solution.py:21
  80.8 0.0 collective-permute-done.6
  80.8 12.2 %fusion.7 = f32[4,16,16,1024]{3,1,2,0:T(8,128)} fusion(f32[4,16,16,1024]{3,1,2,0:T(8,128)S(1)} %fusion.19, f32[4,16,16,1024]{3,1,2,0:T(8,128)S(1)} %fusion.13, f32[4,16,1,1024]{3,1,2,0:T(8,128)S(1)} %collective-permute-done.7, f32[4,16,1,1024]{3,1,2,0:T(8,128)} %collective-permute-done.6, f32[1,16,16,1024]{3,1,2,0:T(8,128)} %get-tuple-element.13, ...), kind=kLoop, calls=%fused_computation.8 | loop fusion | flops 25165824 | bytes 31981588 | tf_op jit(solution)/shard_map/add | solution.py:103
  93.1 3.5 %add_reduce_fusion.1 = (f32[16,1024]{1,0:T(8,128)S(1)}, f32[16,1024]{1,0:T(8,128)S(1)}, f32[16,1024]{1,0:T(8,128)S(1)}) fusion(f32[4,16,16,1024]{3,1,2,0:T(8,128)} %fusion.7, f32[4,16,16,1024]{3,1,2,0:T(8,128)S(1)} %copy_convert_fusion), kind=kLoop, calls=%fused_computation.40 | loop fusion | flops 6242304 | bytes 8585216 | tf_op jit(solution)/shard_map/reduce_sum | solution.py:45
  96.6 0.7 maximum_multiply_fusion.4
  97.3 0.0 all-reduce.2.cloned.1.call-update
  97.3 84.9 %all-reduce.2.cloned.1.call-done = f32[3,16,1024]{2,1,0:T(8,128)} async-done(((f32[3,16,1024]{2,1,0:T(8,128)}), f32[3,16,1024]{2,1,0:T(8,128)}) %all-reduce.2.cloned.1.call-update) | async-done | bytes 196624 | tf_op jit(solution)/shard_map/psum | solution.py:107
  182.2 0.9 subtract_bitcast_fusion.2
  183.1 1.0 multiply_reduce_fusion.1
  184.1 0.4 sqrt_cosine_fusion
  184.5 1.7 fusion.25
  186.2 1.6 copy.12
  (5 shorter events, 0.2 us)
Async XLA Ops:
  7.2 175.0 %all-reduce.2.cloned.1.call-start = ((), (), s32[]{:S(2)}) async-start(), calls=%async_computation | async-start | bytes 393216 | tf_op jit(solution)/shard_map/psum | solution.py:107
  10.1 8.9 %collective-permute-start.1 = (f32[4,16,1,1024]{3,1,2,0:T(8,128)S(1)}, f32[4,16,1,1024]{3,1,2,0:T(8,128)S(1)}, u32[]{:S(2)}, u32[]{:S(2)}) collective-permute-start(f32[4,16,1,1024]{3,1,2,0:T(8,128)S(1)} %get-tuple-element.45), channel_id=1, source_target_pairs={{0,8},{8,16},{16,24},{24,32},{32,40},{40,48},{48,56},{56,64},{64,7... | collective-permute-start | bytes 786440 | tf_op jit(solution)/shard_map/ppermute | solution.py:21
  10.2 6.3 %copy-start.2 = (f32[3,16,1024]{2,1,0:T(8,128)S(1)}, f32[3,16,1024]{2,1,0:T(8,128)}, u32[]{:S(2)}) copy-start(f32[3,16,1024]{2,1,0:T(8,128)} %param.5) | copy-start | bytes 589828
  10.2 6.3 %copy-start.3 = (f32[5]{0:T(128)S(1)}, f32[5]{0:T(128)}, u32[]{:S(2)}) copy-start(f32[5]{0:T(128)} %param.6) | copy-start | bytes 64
  10.2 8.7 %collective-permute-start = (f32[4,16,1,1024]{3,1,2,0:T(8,128)S(1)}, f32[4,16,1,1024]{3,1,2,0:T(8,128)S(1)}, u32[]{:S(2)}, u32[]{:S(2)}) collective-permute-start(f32[4,16,1,1024]{3,1,2,0:T(8,128)S(1)} %get-tuple-element.44), channel_id=1, source_target_pairs={{8,0},{16,8},{24,16},{32,24},{40,32},{48,40},{56,48},{64,56},{72,6... | collective-permute-start | bytes 786440 | tf_op jit(solution)/shard_map/ppermute | solution.py:24
  25.3 12.8 %copy-start.1 = (bf16[4,16,16,1024]{3,2,1,0:T(8,128)(2,1)S(1)}, bf16[4,16,16,1024]{3,2,1,0:T(8,128)(2,1)}, u32[]{:S(2)}) copy-start(bf16[4,16,16,1024]{3,2,1,0:T(8,128)(2,1)} %param.4) | copy-start | bytes 6291460
  28.7 9.4 %collective-permute-start.3 = (f32[4,16,1,1024]{3,1,2,0:T(8,128)S(1)}, f32[4,16,1,1024]{3,1,2,0:T(8,128)S(1)}, u32[]{:S(2)}, u32[]{:S(2)}) collective-permute-start(f32[4,16,1,1024]{3,1,2,0:T(8,128)S(1)} %get-tuple-element.43), channel_id=1, source_target_pairs={{0,8},{8,16},{16,24},{24,32},{32,40},{40,48},{48,56},{56,64},{64,7... | collective-permute-start | bytes 786440 | tf_op jit(solution)/shard_map/ppermute | solution.py:21
  29.8 8.3 %collective-permute-start.2 = (f32[4,16,1,1024]{3,1,2,0:T(8,128)S(1)}, f32[4,16,1,1024]{3,1,2,0:T(8,128)S(1)}, u32[]{:S(2)}, u32[]{:S(2)}) collective-permute-start(f32[4,16,1,1024]{3,1,2,0:T(8,128)S(1)} %get-tuple-element.42), channel_id=1, source_target_pairs={{8,0},{16,8},{24,16},{32,24},{40,32},{48,40},{56,48},{64,56},{72,6... | collective-permute-start | bytes 786440 | tf_op jit(solution)/shard_map/ppermute | solution.py:24
  44.4 14.9 %copy-start = (f32[4,16,16,1024]{3,1,2,0:T(8,128)S(1)}, f32[4,16,16,1024]{3,1,2,0:T(8,128)}, u32[]{:S(2)}) copy-start(f32[4,16,16,1024]{3,1,2,0:T(8,128)} %get-tuple-element.8) | copy-start | bytes 12582916
  49.0 10.3 %collective-permute-start.5 = (f32[4,16,1,1024]{3,1,2,0:T(8,128)S(1)}, f32[4,16,1,1024]{3,1,2,0:T(8,128)S(1)}, u32[]{:S(2)}, u32[]{:S(2)}) collective-permute-start(f32[4,16,1,1024]{3,1,2,0:T(8,128)S(1)} %get-tuple-element.37), channel_id=1, source_target_pairs={{0,8},{8,16},{16,24},{24,32},{32,40},{40,48},{48,56},{56,64},{64,7... | collective-permute-start | bytes 786440 | tf_op jit(solution)/shard_map/ppermute | solution.py:21
  49.1 10.1 %collective-permute-start.4 = (f32[4,16,1,1024]{3,1,2,0:T(8,128)S(1)}, f32[4,16,1,1024]{3,1,2,0:T(8,128)S(1)}, u32[]{:S(2)}, u32[]{:S(2)}) collective-permute-start(f32[4,16,1,1024]{3,1,2,0:T(8,128)S(1)} %get-tuple-element.36), channel_id=1, source_target_pairs={{8,0},{16,8},{24,16},{32,24},{40,32},{48,40},{56,48},{64,56},{72,6... | collective-permute-start | bytes 786440 | tf_op jit(solution)/shard_map/ppermute | solution.py:24
  71.8 9.1 %collective-permute-start.7 = (f32[4,16,1,1024]{3,1,2,0:T(8,128)S(1)}, f32[4,16,1,1024]{3,1,2,0:T(8,128)S(1)}, u32[]{:S(2)}, u32[]{:S(2)}) collective-permute-start(f32[4,16,1,1024]{3,1,2,0:T(8,128)S(1)} %get-tuple-element.31), channel_id=1, source_target_pairs={{0,8},{8,16},{16,24},{24,32},{32,40},{40,48},{48,56},{56,64},{64,7... | collective-permute-start | bytes 786440 | tf_op jit(solution)/shard_map/ppermute | solution.py:21
  71.8 9.1 %collective-permute-start.6 = (f32[4,16,1,1024]{3,1,2,0:T(8,128)S(1)}, f32[4,16,1,1024]{3,1,2,0:T(8,128)}, u32[]{:S(2)}, u32[]{:S(2)}) collective-permute-start(f32[4,16,1,1024]{3,1,2,0:T(8,128)S(1)} %get-tuple-element.30), channel_id=1, source_target_pairs={{8,0},{16,8},{24,16},{32,24},{40,32},{48,40},{56,48},{64,56},{72,6... | collective-permute-start | bytes 786440 | tf_op jit(solution)/shard_map/ppermute | solution.py:24
Sparse Core Ops, SparseCore 0:
  97.4 84.7 all-reduce.1
where the time goes:
time: 195 us
  waiting for transfers between devices  101 us (52%)
  other arithmetic  44.4 us (23%)
  local copies, waits for them, and re-layouts  18.4 us (9%)
  starting transfers between devices  16.3 us (8%)
  between operations  14.8 us (8%)
    psum x1, waiting for transfers between devices, shards(): fields = lax.psum(partial_value, 'vec')  84.9 us
    ppermute x4, waiting for transfers between devices, with_halo(): lax.ppermute(lax.slice_in_dim(block, block.shape[dim] - width, None, axis...  15.8 us
    ppermute x4, starting transfers between devices, with_halo(): lax.ppermute(lax.slice_in_dim(block, 0, width, axis=dim), axis, backward)  14.9 us
    slice x6, local copies, waits for them, and re-layouts, apply_hamiltonian(): jnp.roll(middle, -1, 3)  14.1 us
    add x1, other arithmetic, shards(): moments = moments + coefficients[degree + 1] * following  12.2 us
    sub x2, other arithmetic, shards(): following = 2.0 * following - previous  10.8 us
    add x4, other arithmetic, exchange_term(): spin_z * up_real + spin_x * down_real + spin_y * down_imag  6.17 us
    mul x1, other arithmetic, apply_hamiltonian(): inverse_bound * (coupling * exchange_term(middle, spins_here) - hopping *...  4.23 us
  transfers between devices with their start and end apart: 9, of which 5 were waited for; matrix products, arithmetic and copies ran while one was open for 2% of the time, Pallas kernels for 0%

commit v1 on v0

v1 whole, which is shorter than its diff:
```python
import functools

import jax
import jax.numpy as jnp
from jax import lax
from jax.experimental import pallas as pl
from jax.experimental.pallas import tpu as pltpu
from jax.sharding import PartitionSpec as P

MESH = pl.DeviceIdType.MESH
LAT, VEC = 16, 8
ROWS, COLS, VECS = 16, 1024, 16
BLOCKS = COLS // 128
PAD = 4
coupling = 2.0
inverse_bound = 1.0 / 6.5


def spin_on(state, spin):
    x, y, z = spin
    p0, p1, p2, p3 = state
    return (
        (z * p0 + x * p2) + y * p3,
        (z * p1 + x * p3) - y * p2,
        (x * p0 - y * p1) - z * p2,
        (x * p1 + y * p0) - z * p3,
    )


def density(r, w):
    return (
        (r[0] * w[2] + r[1] * w[3]) + (r[2] * w[0] + r[3] * w[1]),
        (r[0] * w[3] - r[1] * w[2]) - (r[2] * w[1] - r[3] * w[0]),
        (r[0] * w[0] + r[1] * w[1]) - (r[2] * w[2] + r[3] * w[3]),
    )


def lanes(j):
    j = j % BLOCKS
    return slice(j * 128, (j + 1) * 128)


def field_kernel(
    coef, x_hbm, s_vmem, out,
    xv, R, W3, W2, W1, SB, SHs, SHr, D, E, PBs, PBr, FP, RB, SUM,
    xsem, hs, hr, ss, sr, ps, pr, rs_s, rs_r, ag_s, ag_r,
):
    lat, vec = lax.axis_index("lat"), lax.axis_index("vec")
    prev, nxt = lax.rem(lat + LAT - 1, LAT), lax.rem(lat + 1, LAT)

    load = pltpu.make_async_copy(x_hbm, xv, xsem)
    load.start()

    barrier = pltpu.get_barrier_semaphore()
    for to in (prev, nxt):
        pl.semaphore_signal(barrier, 1, device_id={"lat": to}, device_id_type=MESH)
    for d in range(1, VEC):
        pl.semaphore_signal(
            barrier, 1, device_id={"vec": lax.rem(vec + d, VEC)}, device_id_type=MESH
        )

    c0, c1, c2, c3, c4 = (coef[k] for k in range(5))
    h = inverse_bound
    a0 = c0 - c2 + c4
    a1 = (3.0 * c3 - c1) * h
    a2 = (2.0 * c2 - 8.0 * c4) * (h * h)
    a3 = c3 * (-4.0 * h * h * h)
    a4 = c4 * (8.0 * h * h * h * h)

    zero = jnp.zeros((8, COLS), jnp.float32)
    for row in range(ROWS):
        for c in range(3):
            SB[PAD + row, c] = jnp.broadcast_to(2.0 * s_vmem[c, row : row + 1, :], (8, COLS))
    for c in range(3):
        for row in (1, 22):
            SB[row, c] = zero
        for k in range(2):
            q = 2 * c + k
            SHs[0, q : q + 1, :] = s_vmem[c, k : k + 1, :]
            SHs[1, q : q + 1, :] = s_vmem[c, 14 + k : 15 + k, :]
    for s in range(2):
        SHs[s, 6:8, :] = jnp.zeros((2, COLS), jnp.float32)
    for g in range(2):
        for row in (0, 1, 22, 23):
            for c in range(4):
                R[g, row, c] = zero
        for s in range(2):
            for j in range(BLOCKS):
                E[s, g, j, 48:64, :] = jnp.zeros((16, 128), jnp.float32)

    m = lax.broadcasted_iota(jnp.int32, (256, 256), 0)
    k = lax.broadcasted_iota(jnp.int32, (256, 256), 1)
    swap = jnp.where((k % 16 == m // 16) & (k // 16 == m % 16), 1.0, 0.0).astype(jnp.bfloat16)
    load.wait()

    @pl.loop(0, 4)
    def _(c):
        for q in range(4):
            cols = slice(q * 256, (q + 1) * 256)
            got = jnp.dot(
                swap, xv[c, :, :, cols].reshape(256, 256), preferred_element_type=jnp.float32
            )
            for row in range(ROWS):
                for g in range(2):
                    R[g, PAD + row, c, :, cols] = got[row * 16 + g * 8 : row * 16 + g * 8 + 8]

    pl.semaphore_wait(barrier, 2 + VEC - 1)

    def spin_copy(s):
        return pltpu.make_async_remote_copy(
            SHs.at[s], SHr.at[1 - s], ss.at[s], sr.at[1 - s],
            device_id={"lat": (prev, nxt)[s]}, device_id_type=MESH,
        )

    def halo_copy(s, g):
        src, dst = ((4, 20), (18, 2))[s]
        return pltpu.make_async_remote_copy(
            R.at[g, pl.ds(src, 2)], R.at[g, pl.ds(dst, 2)], hs.at[s, g], hr.at[1 - s, g],
            device_id={"lat": (prev, nxt)[s]}, device_id_type=MESH,
        )

    for s in range(2):
        spin_copy(s).start()
    for g in range(2):
        for s in range(2):
            halo_copy(s, g).start()

    lane = lax.broadcasted_iota(jnp.int32, (8, 128), 1)
    first, last = lane == 0, lane == 127

    def around(ref, at, j):
        here = ref[at + (slice(None), lanes(j))]
        left = jnp.where(last, ref[at + (slice(None), lanes(j - 1))], here)
        right = jnp.where(first, ref[at + (slice(None), lanes(j + 1))], here)
        return pltpu.roll(left, 1, 1) + pltpu.roll(right, 127, 1)

    def hop(src, g, row, j):
        cols = (slice(None), lanes(j))
        spin = [SB[(PAD + row, c) + cols] for c in range(3)]
        state = [src[(g, PAD + row, c) + cols] for c in range(4)]
        onsite = spin_on(state, spin)
        res = []
        for c in range(4):
            n = src[(g, PAD + row - 1, c) + cols] + src[(g, PAD + row + 1, c) + cols]
            res.append((n + around(src, (g, PAD + row, c), j)) - onsite[c])
        return res

    def sweep(g, starts, counts, slot_shift):
        @pl.loop(0, counts[0])
        def _(i):
            row = starts[0] + i
            for j in range(BLOCKS):
                cols = (slice(None), lanes(j))
                got = hop(R, g, row, j)
                for c in range(4):
                    W3[(g, PAD + row, c) + cols] = a4 * got[c] + a3 * R[(g, PAD + row, c) + cols]

        for level, (src, dst, a) in enumerate(((W3, W2, a2), (W2, W1, a1)), 1):
            @pl.loop(0, counts[level])
            def _(i):
                row = starts[level] + i
                for j in range(BLOCKS):
                    cols = (slice(None), lanes(j))
                    got = hop(src, g, row, j)
                    for c in range(4):
                        dst[(g, PAD + row, c) + cols] = got[c] + a * R[(g, PAD + row, c) + cols]

        @pl.loop(0, counts[3])
        def _(i):
            row = starts[3] + i
            at = pl.multiple_of((row + slot_shift) * 8, 8)
            for j in range(BLOCKS):
                cols = (slice(None), lanes(j))
                got = hop(W1, g, row, j)
                r = [R[(g, PAD + row, c) + cols] for c in range(4)]
                w = [got[c] + a0 * r[c] for c in range(4)]
                for c, d in enumerate(density(r, w)):
                    D[g, c, j, pl.ds(at, 8), :] = d

    def fold(ref, at, start):
        parts = []
        for g in range(2):
            for s in range(8):
                parts.append(ref[at(g) + (pl.ds(start + s, 8, stride=8), slice(None))])
        while len(parts) > 1:
            parts = [parts[i] + parts[i + 1] for i in range(0, len(parts), 2)]
        return parts[0]

    def scatter_copy(grp, d):
        to = lax.rem(vec + d, VEC)
        return pltpu.make_async_remote_copy(
            FP.at[grp, to], RB.at[grp, d], rs_s.at[grp, d], rs_r.at[grp, d],
            device_id={"vec": to}, device_id_type=MESH,
        )

    def gather_copy(grp, d):
        to = lax.rem(vec + d, VEC)
        return pltpu.make_async_remote_copy(
            SUM.at[grp], out.at[grp, vec], ag_s.at[grp, d], ag_r.at[grp, d],
            device_id={"vec": to}, device_id_type=MESH,
        )

    def reduce_and_gather(grp):
        for d in range(1, VEC):
            scatter_copy(grp, d).wait_recv()
        for c in range(3):
            total = FP[grp, vec, c]
            for d in range(1, VEC):
                total = total + RB[grp, d, c]
            SUM[grp, c] = total
            out[grp, vec, c] = total
        for d in range(1, VEC):
            gather_copy(grp, d).start()

    @pl.loop(0, 2)
    def _(g):
        sweep(g, (1, 2, 3, 4), (14, 12, 10, 8), -4)

    @pl.loop(0, BLOCKS)
    def _(j):
        for c in range(3):
            FP[0, j, c] = fold(D, lambda g: (g, c, j), 0)
    for d in range(1, VEC):
        scatter_copy(0, d).start()

    for s in range(2):
        spin_copy(s).wait()
    for s in range(2):
        for c in range(3):
            for k in range(2):
                q = 2 * c + k
                SB[(2, 20)[s] + k, c] = jnp.broadcast_to(2.0 * SHr[s, q : q + 1, :], (8, COLS))

    def push(s, g):
        far, near = 2 + 11 * s + PAD, PAD - 1 + 17 * s
        row_far, row_next = PAD - 2 + 19 * s, PAD + 3 + 9 * s
        base = PAD - 1 + 14 * s
        at0 = [pl.multiple_of((2 * c + 1 - s) * 8, 8) for c in range(3)]
        at1 = [pl.multiple_of((2 * c + s) * 8, 8) for c in range(3)]
        for j in range(BLOCKS):
            cols = (slice(None), lanes(j))
            spin = [
                (SB[(base, c) + cols] + SB[(base + 1, c) + cols])
                + (SB[(base + 2, c) + cols] + SB[(base + 3, c) + cols])
                for c in range(3)
            ]
            b2 = [R[(g, far, c) + cols] for c in range(4)]
            onsite = spin_on(b2, spin)
            u, v = [], []
            for c in range(4):
                more = R[(g, row_next, c) + cols] + 4.0 * around(R, (g, far, c), j)
                u.append(a3 * b2[c] + a4 * (more - onsite[c]))
                v.append(a4 * b2[c])
            r0 = [R[(g, near, c) + cols] for c in range(4)]
            r1 = [R[(g, row_far, c) + cols] for c in range(4)]
            for c, d in enumerate(density(r0, u)):
                E[s, g, j, pl.ds(at0[c], 8), :] = d
            for c, d in enumerate(density(r1, v)):
                E[s, g, j, pl.ds(at1[c], 8), :] = d

    def wait_halo(s, g):
        pltpu.make_async_copy(R.at[g, pl.ds(2, 2)], R.at[g, pl.ds(2, 2)], hr.at[s, g]).wait()

    def push_copy(s):
        return pltpu.make_async_remote_copy(
            PBs.at[s], PBr.at[1 - s], ps.at[s], pr.at[1 - s],
            device_id={"lat": lax.rem(lat + LAT - 1 + 2 * s, LAT)}, device_id_type=MESH,
        )

    def wedge(s, g):
        sweep(g, (18 * s - 3, 16 * s - 2, 14 * s - 1, 12 * s), (4, 4, 4, 4), 12 - 16 * s)

    near_side = 1 - lax.rem(lat, 2)
    for s in (near_side, 1 - near_side):
        wait_halo(s, 0)
        push(s, 0)
        wedge(s, 0)
        wait_halo(s, 1)
        push(s, 1)

        @pl.loop(0, BLOCKS)
        def _(j):
            PBs[s, j] = fold(E, lambda g: (s, g, j), 0)

        push_copy(s).start()
        wedge(s, 1)

    reduce_and_gather(0)

    for s in range(2):
        push_copy(s).wait()

    sub = lax.broadcasted_iota(jnp.int32, (8, 128), 0)
    from_next, from_prev = (sub == 2) | (sub == 3), (sub == 4) | (sub == 5)

    @pl.loop(0, BLOCKS)
    def _(j):
        for c in range(3):
            total = fold(D, lambda g: (g, c, j), 64)
            total = total + jnp.where(from_next, pltpu.roll(PBr[1, j], (2 - 2 * c) % 8, 0), 0.0)
            total = total + jnp.where(from_prev, pltpu.roll(PBr[0, j], (4 - 2 * c) % 8, 0), 0.0)
            FP[1, j, c] = total

    for d in range(1, VEC):
        scatter_copy(1, d).start()
    reduce_and_gather(1)

    for s in range(2):
        for g in range(2):
            halo_copy(s, g).wait_send()
    for grp in range(2):
        for d in range(1, VEC):
            scatter_copy(grp, d).wait_send()
            gather_copy(grp, d).wait()


def rotate_kernel(f_ref, s_ref, rot, fields):
    sub = lax.broadcasted_iota(jnp.int32, (8, 128), 0)
    top = sub < 4
    for j in range(BLOCKS):
        cols = lanes(j)
        mid = [pltpu.roll(f_ref[0, j, c], 4, 0) for c in range(3)]
        edge = [pltpu.roll(f_ref[1, j, c], 4, 0) for c in range(3)]
        for half in range(2):
            rows = slice(half * 8, half * 8 + 8)
            a, b = (edge, mid) if half == 0 else (mid, edge)
            B = [jnp.where(top, a[c], b[c]) * (coupling / (VECS * VEC)) for c in range(3)]
            S = [s_ref[c, rows, cols] for c in range(3)]
            square = B[0] * B[0] + B[1] * B[1] + B[2] * B[2]
            size = jnp.sqrt(square)
            half_angle = 0.5 * size
            sin_h, cos_h = jnp.sin(half_angle), jnp.cos(half_angle)
            some = size > 0.0
            safe = jnp.where(some, size, 1.0)
            ratio = jnp.where(some, sin_h / safe, 0.5)
            cosine = 1.0 - 2.0 * (sin_h * sin_h)
            sine_ratio = 2.0 * (ratio * cos_h)
            along = 2.0 * (ratio * ratio) * (B[0] * S[0] + B[1] * S[1] + B[2] * S[2])
            cross = (
                B[1] * S[2] - B[2] * S[1],
                B[2] * S[0] - B[0] * S[2],
                B[0] * S[1] - B[1] * S[0],
            )
            for c in range(3):
                fields[c, rows, cols] = B[c]
                rot[c, rows, cols] = (cosine * S[c] + sine_ratio * cross[c]) + along * B[c]


def shards(vectors, classical_spins, coefficients):
    f32 = jnp.float32
    vmem = pl.BlockSpec(memory_space=pltpu.VMEM)
    dma = pltpu.SemaphoreType.DMA
    parts = pl.pallas_call(
        field_kernel,
        name="fields",
        out_shape=jax.ShapeDtypeStruct((2, BLOCKS, 3, 8, 128), f32),
        in_specs=[
            pl.BlockSpec(memory_space=pltpu.SMEM),
            pl.BlockSpec(memory_space=pl.ANY),
            vmem,
        ],
        out_specs=vmem,
        scratch_shapes=[
            pltpu.VMEM((4, VECS, ROWS, COLS), jnp.bfloat16),
            *[pltpu.VMEM((2, 24, 4, 8, COLS), f32)] * 4,
            pltpu.VMEM((24, 3, 8, COLS), f32),
            pltpu.VMEM((2, 8, COLS), f32),
            pltpu.VMEM((2, 8, COLS), f32),
            pltpu.VMEM((2, 3, BLOCKS, 128, 128), f32),
            pltpu.VMEM((2, 2, BLOCKS, 64, 128), f32),
            pltpu.VMEM((2, BLOCKS, 8, 128), f32),
            pltpu.VMEM((2, BLOCKS, 8, 128), f32),
            pltpu.VMEM((2, BLOCKS, 3, 8, 128), f32),
            pltpu.VMEM((2, VEC, 3, 8, 128), f32),
            pltpu.VMEM((2, 3, 8, 128), f32),
            dma, dma((2, 2)), dma((2, 2)), dma((2,)), dma((2,)), dma((2,)), dma((2,)),
            dma((2, VEC)), dma((2, VEC)), dma((2, VEC)), dma((2, VEC)),
        ],
        compiler_params=pltpu.CompilerParams(
            collective_id=0, has_side_effects=True, vmem_limit_bytes=60 << 20
        ),
    )(coefficients, vectors, classical_spins)
    out = jax.ShapeDtypeStruct((3, ROWS, COLS), f32)
    rotated, fields = pl.pallas_call(
        rotate_kernel,
        name="rotate",
        out_shape=(out, out),
        in_specs=[vmem, vmem],
        out_specs=(vmem, vmem),
    )(parts, classical_spins)
    return rotated, fields


def solution(mesh):
    placed = (P(None, "vec", "lat", None), P(None, "lat", None), P())
    return jax.shard_map(
        shards,
        mesh=mesh,
        in_specs=placed,
        out_specs=(P(None, "lat", None), P(None, "lat", None)),
        check_vma=False,
    )
```

time: 195 us -> 46.3 us (0.24)
  waiting for transfers between devices: 101 us -> 0 us
  Pallas kernels: 0 us -> 45.5 us
  other arithmetic: 44.4 us -> 0 us
  local copies, waits for them, and re-layouts: 18.4 us -> 0 us
  starting transfers between devices: 16.3 us -> 0 us
  between operations: 14.8 us -> 0.64 us
    psum x1 -> x0, waiting for transfers between devices: 84.9 us -> none  [shards(): fields = lax.psum(partial_value, 'vec')]
    pallas_call x0 -> x2, Pallas kernels: none -> 45.5 us  [the longest x1 43.4 us: shards(): pl.pallas_call(field_kernel, name='fields', out_shape=jax.ShapeDtypeStruc...]
    add x6 -> x0, other arithmetic: 20 us -> none  [the longest x1 12.2 us: shards(): moments = moments + coefficients[degree + 1] * following]
    slice x13 -> x0, local copies, waits for them, and re-layouts: 16.8 us -> none  [the longest x6 14.1 us: apply_hamiltonian(): jnp.roll(middle, -1, 3)]
    ppermute x8 -> x0, starting transfers between devices: 16.2 us -> none  [the longest x4 14.9 us: with_halo(): lax.ppermute(lax.slice_in_dim(block, 0, width, axis=dim), axis, backward)]
    ppermute x8 -> x0, waiting for transfers between devices: 15.8 us -> none  [the longest x4 15.8 us: with_halo(): lax.ppermute(lax.slice_in_dim(block, block.shape[dim] - width, None, axis...]
    sub x3 -> x0, other arithmetic: 11.8 us -> none  [the longest x2 10.8 us: shards(): following = 2.0 * following - previous]
    mul x2 -> x0, other arithmetic: 4.92 us -> none  [the longest x1 4.23 us: apply_hamiltonian(): inverse_bound * (coupling * exchange_term(middle, spins_here) - hopping *...]
  transfers between devices with their start and end apart: 9 -> 0, of which waited for: 5 -> 0; matrix products, arithmetic and copies ran while one was open for 2% -> 0% of each run, Pallas kernels for 0% -> 0%
where the time goes in v1:
time: 46.3 us; the launch traced here: 46.1 us
  Pallas kernels  45.5 us (98%)
  between operations  0.64 us (1%)
    pallas_call x1, Pallas kernels, shards(): pl.pallas_call(field_kernel, name='fields', out_shape=jax.ShapeDtypeStruc...  43.4 us
    pallas_call x1, Pallas kernels, shards(): pl.pallas_call(rotate_kernel, name='rotate', out_shape=(out, out), in_spe...  2.1 us

profile of v1, /device:TPU:0, one launch (start us, length us, event | category | flops | bytes accessed | tf_op | source)
XLA Modules:
  0.0 46.1 jit_solution(11716107189516445162)
XLA Ops:
  0.6 43.4 %fields.1.f_ref = f32[2,8,3,8,128]{4,3,2,1,0:T(8,128)} custom-call(f32[5]{0:T(128)} %coef.1, bf16[4,16,16,1024]{3,2,1,0:T(8,128)(2,1)} %x_hbm.1, f32[3,16,1024]{2,1,0:T(8,128)} %s_ref.1), custom_call_target="tpu_custom_call" | custom-call | tf_op jit(solution)/shard_map/fields/pallas_call | solution.py:353
  44.0 2.1 %rotate.1 = (f32[3,16,1024]{2,1,0:T(8,128)}, f32[3,16,1024]{2,1,0:T(8,128)}) custom-call(f32[2,8,3,8,128]{4,3,2,1,0:T(8,128)} %fields.1.f_ref, f32[3,16,1024]{2,1,0:T(8,128)} %s_ref.1), custom_call_target="tpu_custom_call" | custom-call | tf_op jit(solution)/shard_map/rotate/pallas_call | solution.py:384

commit v2 on v1

v2 whole, which is shorter than its diff:
```python
import functools

import jax
import jax.numpy as jnp
from jax import lax
from jax.experimental import pallas as pl
from jax.experimental.pallas import tpu as pltpu
from jax.sharding import PartitionSpec as P

MESH = pl.DeviceIdType.MESH
LAT, VEC, NY = 16, 8, 4
ROWS, COLS, VECS = 16, 1024, 16
BLOCKS = COLS // 128
PAD = 4
STEPS_EACH = 4
coupling = 2.0
inverse_bound = 1.0 / 6.5


def spin_on(state, spin):
    x, y, z = spin
    p0, p1, p2, p3 = state
    return (
        (z * p0 + x * p2) + y * p3,
        (z * p1 + x * p3) - y * p2,
        (x * p0 - y * p1) - z * p2,
        (x * p1 + y * p0) - z * p3,
    )


def density(r, w):
    return (
        (r[0] * w[2] + r[1] * w[3]) + (r[2] * w[0] + r[3] * w[1]),
        (r[0] * w[3] - r[1] * w[2]) - (r[2] * w[1] - r[3] * w[0]),
        (r[0] * w[0] + r[1] * w[1]) - (r[2] * w[2] + r[3] * w[3]),
    )


def bf16_parts(x):
    high = x.astype(jnp.bfloat16)
    rest = x - high.astype(jnp.float32)
    mid = rest.astype(jnp.bfloat16)
    low = (rest - mid.astype(jnp.float32)).astype(jnp.bfloat16)
    return jnp.concatenate([high, mid, low], axis=0)


def permuted(x, by):
    n = x.shape[0]
    got = jnp.dot(bf16_parts(x), by, preferred_element_type=jnp.float32)
    return (got[:n] + got[n : 2 * n]) + got[2 * n :]


def deal(inverse=False):
    here = lax.broadcasted_iota(jnp.int32, (256, 256), int(inverse))
    there = lax.broadcasted_iota(jnp.int32, (256, 256), int(not inverse))
    source = jnp.where(there < 128, 2 * there, 2 * there - 255)
    return jnp.where(here == source, 1.0, 0.0).astype(jnp.bfloat16)


def lanes(j):
    j = j % BLOCKS
    return slice(j * 128, (j + 1) * 128)


def field_kernel(
    coef, x_hbm, s_vmem, out_mid, out_edge,
    xv, R, W3, W2, W1, SB, SHs, SHr, DM, DE, E, PBs, PBr,
    FM, RM, QM, XM, FE, RE, QE, XE, SP, RB,
    xsem, hs, hr, ss, sr, ps, pr, ys_s, ys_r, xs_s, xs_r, yg_s, yg_r, bs_s, bs_r,
):
    lat, vec = lax.axis_index("lat"), lax.axis_index("vec")
    prev, nxt = lax.rem(lat + LAT - 1, LAT), lax.rem(lat + 1, LAT)
    y = lax.rem(vec, NY)
    base = vec - y
    partner = lax.rem(vec + NY, VEC)

    def y_peer(d):
        return base + lax.rem(y + d, NY)

    load = pltpu.make_async_copy(x_hbm, xv, xsem)
    load.start()

    barrier = pltpu.get_barrier_semaphore()
    for to in (prev, nxt):
        pl.semaphore_signal(barrier, 1, device_id={"lat": to}, device_id_type=MESH)
    for to in (y_peer(1), y_peer(2), y_peer(3), partner):
        pl.semaphore_signal(barrier, 1, device_id={"vec": to}, device_id_type=MESH)

    c0, c1, c2, c3, c4 = (coef[k] for k in range(5))
    h = inverse_bound
    a0 = c0 - c2 + c4
    a1 = (3.0 * c3 - c1) * h
    a2 = (2.0 * c2 - 8.0 * c4) * (h * h)
    a3 = c3 * (-4.0 * h * h * h)
    a4 = c4 * (8.0 * h * h * h * h)

    by_deal = deal()
    for q in range(4):
        cols = slice(q * 256, (q + 1) * 256)
        SP[:, cols] = permuted(s_vmem[:, :, cols].reshape(3 * ROWS, 256), by_deal)
    for c in range(3):
        for k in range(2):
            q, at = 2 * c + k, c * ROWS + k
            SHs[0, q : q + 1, :] = SP[at : at + 1, :]
            SHs[1, q : q + 1, :] = SP[at + 14 : at + 15, :]
    for s in range(2):
        SHs[s, 6:8, :] = jnp.zeros((2, COLS), jnp.float32)
    zero = jnp.zeros((8, COLS), jnp.float32)
    for row in range(ROWS):
        for c in range(3):
            at = c * ROWS + row
            SB[PAD + row, c] = jnp.broadcast_to(2.0 * SP[at : at + 1, :], (8, COLS))

    def swap(order):
        n = 16 * len(order)
        m = lax.broadcasted_iota(jnp.int32, (n, 256), 0)
        k = lax.broadcasted_iota(jnp.int32, (n, 256), 1)
        at = m // 16
        row = jnp.where(at < 2, at, at + 12) if order[0] == 0 else at + 2
        return jnp.where((k % 16 == row) & (k // 16 == m % 16), 1.0, 0.0).astype(jnp.bfloat16)

    def spread(order):
        by = swap(order)

        @pl.loop(0, 4)
        def _(c):
            for q in range(4):
                cols = slice(q * 256, (q + 1) * 256)
                got = jnp.dot(
                    by, xv[c, :, :, cols].reshape(256, 256), preferred_element_type=jnp.float32
                ).astype(jnp.bfloat16)
                got = jnp.dot(got, by_deal, preferred_element_type=jnp.float32)
                for at, row in enumerate(order):
                    for g in range(2):
                        lo = at * 16 + g * 8
                        R[g, PAD + row, c, :, cols] = got[lo : lo + 8]

    load.wait()
    spread((0, 1, 14, 15))
    pl.semaphore_wait(barrier, 2 + 4)

    def spin_copy(s):
        return pltpu.make_async_remote_copy(
            SHs.at[s], SHr.at[1 - s], ss.at[s], sr.at[1 - s],
            device_id={"lat": (prev, nxt)[s]}, device_id_type=MESH,
        )

    def halo_copy(s, g):
        src, dst = ((4, 20), (18, 2))[s]
        return pltpu.make_async_remote_copy(
            R.at[g, pl.ds(src, 2)], R.at[g, pl.ds(dst, 2)], hs.at[s, g], hr.at[1 - s, g],
            device_id={"lat": (prev, nxt)[s]}, device_id_type=MESH,
        )

    for s in range(2):
        spin_copy(s).start()
    for g in range(2):
        for s in range(2):
            halo_copy(s, g).start()

    spread(tuple(range(2, 14)))
    for c in range(3):
        for row in (1, 22):
            SB[row, c] = zero
    for g in range(2):
        for row in (0, 1, 22, 23):
            for c in range(4):
                R[g, row, c] = zero
        for s in range(2):
            for j in range(BLOCKS):
                E[s, g, j, 48:64, :] = jnp.zeros((16, 128), jnp.float32)

    lane = lax.broadcasted_iota(jnp.int32, (8, 128), 1)
    first, last = lane == 0, lane == 127

    def around(ref, at, j):
        other = ref[at + (slice(None), lanes(j ^ 1))]
        if j % 2 == 0:
            return other + pltpu.roll(
                jnp.where(last, ref[at + (slice(None), lanes(j - 1))], other), 1, 1
            )
        return other + pltpu.roll(
            jnp.where(first, ref[at + (slice(None), lanes(j + 1))], other), 127, 1
        )

    def hop(src, g, row, j):
        cols = (slice(None), lanes(j))
        spin = [SB[(PAD + row, c) + cols] for c in range(3)]
        state = [src[(g, PAD + row, c) + cols] for c in range(4)]
        onsite = spin_on(state, spin)
        res = []
        for c in range(4):
            n = src[(g, PAD + row - 1, c) + cols] + src[(g, PAD + row + 1, c) + cols]
            res.append((n + around(src, (g, PAD + row, c), j)) - onsite[c])
        return res

    def steps(groups, start, count, body):
        each = STEPS_EACH // len(groups)

        @pl.loop(0, count // each)
        def _(i):
            for k in range(each):
                for g in groups:
                    body(g, start + each * i + k)

    def sweep(groups, starts, counts, keep):
        def third(g, row):
            for j in range(BLOCKS):
                cols = (slice(None), lanes(j))
                got = hop(R, g, row, j)
                for c in range(4):
                    W3[(g, PAD + row, c) + cols] = a4 * got[c] + a3 * R[(g, PAD + row, c) + cols]

        steps(groups, starts[0], counts[0], third)

        for level, (src, dst, a) in enumerate(((W3, W2, a2), (W2, W1, a1)), 1):
            def lower(g, row):
                for j in range(BLOCKS):
                    cols = (slice(None), lanes(j))
                    got = hop(src, g, row, j)
                    for c in range(4):
                        dst[(g, PAD + row, c) + cols] = got[c] + a * R[(g, PAD + row, c) + cols]

            steps(groups, starts[level], counts[level], lower)

        def finish(g, row):
            for j in range(BLOCKS):
                cols = (slice(None), lanes(j))
                got = hop(W1, g, row, j)
                r = [R[(g, PAD + row, c) + cols] for c in range(4)]
                w = [got[c] + a0 * r[c] for c in range(4)]
                for c, d in enumerate(density(r, w)):
                    keep(g, c, j, row, d)

        steps(groups, starts[3], counts[3], finish)

    def fold(ref, at):
        parts = []
        for g in range(2):
            for s in range(8):
                parts.append(ref[at(g) + (pl.ds(s, 8, stride=8), slice(None))])
        while len(parts) > 1:
            parts = [parts[i] + parts[i + 1] for i in range(0, len(parts), 2)]
        return parts[0]

    def refs(grp, mid, edge):
        return mid if grp is None else edge.at[grp]

    def sem(ref, grp, *at):
        return ref.at[(0 if grp is None else 1 + grp, *at)]

    def y_scatter(grp, d):
        to = y_peer(d)
        return pltpu.make_async_remote_copy(
            refs(grp, FM, FE).at[to - base], refs(grp, RM, RE).at[d],
            sem(ys_s, grp, d), sem(ys_r, grp, d),
            device_id={"vec": to}, device_id_type=MESH,
        )

    def x_exchange(grp):
        return pltpu.make_async_remote_copy(
            refs(grp, QM, QE), refs(grp, XM, XE), sem(xs_s, grp), sem(xs_r, grp),
            device_id={"vec": partner}, device_id_type=MESH,
        )

    def y_gather(grp, d):
        here = refs(grp, out_mid, out_edge).at[y]
        return pltpu.make_async_remote_copy(
            here, here, sem(yg_s, grp, d), sem(yg_r, grp, d),
            device_id={"vec": y_peer(d)}, device_id_type=MESH,
        )

    def scatter(grp):
        for d in range(1, NY):
            y_scatter(grp, d).start()

    def exchange(grp):
        for d in range(1, NY):
            y_scatter(grp, d).wait_recv()
        got, mine = refs(grp, RM, RE), refs(grp, FM, FE)
        total = (mine[y] + got[1]) + (got[2] + got[3])
        into = refs(grp, QM, QE)
        if grp is None:
            into[...] = total
        else:
            for d in range(NY):
                chip_push(d).wait_recv()
            extra = placed(grp, NY)
            for c in range(3):
                into[c] = total[c] + extra[c]
        x_exchange(grp).start()

    def gather(grp):
        x_exchange(grp).wait_recv()
        refs(grp, out_mid, out_edge)[y] = refs(grp, QM, QE)[...] + refs(grp, XM, XE)[...]
        for d in range(1, NY):
            y_gather(grp, d).start()

    def keep_mid(g, c, j, row, d):
        at = pl.multiple_of((row - 4) * 8, 8)
        DM[g, c, j, pl.ds(at, 8), :] = d

    def keep_edge(s):
        def keep(g, c, j, row, d):
            at = pl.multiple_of(lax.rem(row + 2 * s, 4) * 8 + 32 * (j % 2), 8)
            DE[s, g, c, j // 2, pl.ds(at, 8), :] = d

        return keep

    sweep((0, 1), (1, 2, 3, 4), (14, 12, 10, 8), keep_mid)

    @pl.loop(0, NY)
    def _(q):
        for half in range(2):
            for c in range(3):
                FM[q, half, c] = fold(DM, lambda g: (g, c, 2 * q + half))

    scatter(None)

    for s in range(2):
        spin_copy(s).wait()
    for s in range(2):
        for c in range(3):
            for k in range(2):
                q = 2 * c + k
                SB[(2, 20)[s] + k, c] = jnp.broadcast_to(2.0 * SHr[s, q : q + 1, :], (8, COLS))

    def push(s, g):
        far, near = 2 + 11 * s + PAD, PAD - 1 + 17 * s
        row_far, row_next = PAD - 2 + 19 * s, PAD + 3 + 9 * s
        low = PAD - 1 + 14 * s
        at0 = [pl.multiple_of((2 * c + 1 - s) * 8, 8) for c in range(3)]
        at1 = [pl.multiple_of((2 * c + s) * 8, 8) for c in range(3)]
        for j in range(BLOCKS):
            cols = (slice(None), lanes(j))
            spin = [
                (SB[(low, c) + cols] + SB[(low + 1, c) + cols])
                + (SB[(low + 2, c) + cols] + SB[(low + 3, c) + cols])
                for c in range(3)
            ]
            b2 = [R[(g, far, c) + cols] for c in range(4)]
            onsite = spin_on(b2, spin)
            u, v = [], []
            for c in range(4):
                more = R[(g, row_next, c) + cols] + 4.0 * around(R, (g, far, c), j)
                u.append(a3 * b2[c] + a4 * (more - onsite[c]))
                v.append(a4 * b2[c])
            r0 = [R[(g, near, c) + cols] for c in range(4)]
            r1 = [R[(g, row_far, c) + cols] for c in range(4)]
            for c, d in enumerate(density(r0, u)):
                E[s, g, j, pl.ds(at0[c], 8), :] = d
            for c, d in enumerate(density(r1, v)):
                E[s, g, j, pl.ds(at1[c], 8), :] = d

    def wait_halo(s, g):
        pltpu.make_async_copy(R.at[g, pl.ds(2, 2)], R.at[g, pl.ds(2, 2)], hr.at[s, g]).wait()

    chip_side = 1 - lax.rem(lat, 2)
    link_side = 1 - chip_side

    def beyond(s):
        return lax.rem(lat + LAT - 1 + 2 * s, LAT)

    def chip_push(d):
        to = y_peer(d)
        return pltpu.make_async_remote_copy(
            PBs.at[chip_side, pl.ds(2 * (to - base), 2)], PBr.at[1 - chip_side, d],
            ps.at[0, d], pr.at[0, d],
            device_id={"lat": beyond(chip_side), "vec": to}, device_id_type=MESH,
        )

    def link_push(d):
        to = lax.rem(vec + d, VEC)
        return pltpu.make_async_remote_copy(
            PBs.at[link_side, pl.ds(2 * lax.rem(to, NY), 2)], PBr.at[1 - link_side, d],
            ps.at[1, d], pr.at[1, d],
            device_id={"lat": beyond(link_side), "vec": to}, device_id_type=MESH,
        )

    def link_scatter(d):
        to = lax.rem(vec + d, VEC)
        return pltpu.make_async_remote_copy(
            FE.at[link_side, lax.rem(to, NY)], RB.at[d], bs_s.at[d], bs_r.at[d],
            device_id={"vec": to}, device_id_type=MESH,
        )

    sub = lax.broadcasted_iota(jnp.int32, (8, 128), 0)

    def placed(s, count):
        got = PBr[s, 0]
        for d in range(1, count):
            got = got + PBr[s, d]
        res = []
        for c in range(3):
            total = jnp.zeros((8, 128), jnp.float32)
            for half in range(2):
                here = (sub == 4 * half) | (sub == 4 * half + 1)
                moved = pltpu.roll(got[half], (4 * half - 2 * c) % 8, 0)
                total = jnp.where(here, moved, total)
            res.append(total)
        return res

    def wedge(s, groups):
        sweep(
            groups, (18 * s - 3, 16 * s - 2, 14 * s - 1, 12 * s), (4, 4, 4, 4), keep_edge(s)
        )

    def fold_push(s):
        @pl.loop(0, BLOCKS)
        def _(j):
            PBs[s, j] = fold(E, lambda g: (s, g, j))

    def fold_edge(s):
        @pl.loop(0, NY)
        def _(q):
            for c in range(3):
                FE[s, q, c] = fold(DE, lambda g: (s, g, c, q))

    s = chip_side
    for g in range(2):
        wait_halo(s, g)
    wedge(s, (0, 1))
    exchange(None)
    for g in range(2):
        push(s, g)
    fold_push(s)
    for d in range(NY):
        chip_push(d).start()
    fold_edge(s)
    scatter(s)

    s = link_side
    wait_halo(s, 0)
    push(s, 0)
    wedge(s, (0,))
    gather(None)
    exchange(chip_side)
    wait_halo(s, 1)
    push(s, 1)
    fold_push(s)
    for d in range(VEC):
        link_push(d).start()
    wedge(s, (1,))
    fold_edge(s)
    for d in range(1, VEC):
        link_scatter(d).start()
    gather(chip_side)
    for d in range(1, VEC):
        link_scatter(d).wait_recv()
    for d in range(VEC):
        link_push(d).wait_recv()
    extra = placed(s, VEC)
    for c in range(3):
        total = FE[s, y, c] + extra[c]
        for d in range(1, VEC):
            total = total + RB[d, c]
        out_edge[s, y, c] = total
    for d in range(1, NY):
        y_gather(s, d).start()

    for s in range(2):
        for g in range(2):
            halo_copy(s, g).wait_send()
    for d in range(NY):
        chip_push(d).wait_send()
    for d in range(VEC):
        link_push(d).wait_send()
    for d in range(1, VEC):
        link_scatter(d).wait_send()
    for grp in (None, chip_side):
        x_exchange(grp).wait_send()
        for d in range(1, NY):
            y_scatter(grp, d).wait_send()
            y_gather(grp, d).wait()
    for d in range(1, NY):
        y_gather(link_side, d).wait()


def rotate_kernel(mid_ref, edge_ref, s_ref, rot, fields):
    sub = lax.broadcasted_iota(jnp.int32, (8, 128), 0)
    top, third = sub < 4, sub < 6
    by = deal(inverse=True)
    dealt = [[] for _ in range(BLOCKS)]
    for j in range(BLOCKS):
        q, half = divmod(j, 2)
        low, high = [], []
        for c in range(3):
            mid = pltpu.roll(mid_ref[q, half, c], 4, 0)
            start, end = edge_ref[0, q, c], edge_ref[1, q, c]
            if half:
                start = pltpu.roll(start, 4, 0)
            end = jnp.where(
                third,
                pltpu.roll(end, (2 - 4 * half) % 8, 0),
                pltpu.roll(end, (6 - 4 * half) % 8, 0),
            )
            low.append(jnp.where(top, start, mid))
            high.append(jnp.where(top, mid, end))
        dealt[j] = jnp.concatenate(low + high, axis=0) * (coupling / (VECS * VEC))
    for j in range(BLOCKS):
        if j % 2 == 0:
            natural = permuted(jnp.concatenate(dealt[j : j + 2], axis=1), by)
        cols = lanes(j)
        for block in range(2):
            rows = slice(block * 8, block * 8 + 8)
            at = (j % 2) * 128
            B = [
                natural[(3 * block + c) * 8 : (3 * block + c + 1) * 8, at : at + 128]
                for c in range(3)
            ]
            S = [s_ref[c, rows, cols] for c in range(3)]
            square = B[0] * B[0] + B[1] * B[1] + B[2] * B[2]
            size = jnp.sqrt(square)
            half_angle = 0.5 * size
            sin_h, cos_h = jnp.sin(half_angle), jnp.cos(half_angle)
            some = size > 0.0
            safe = jnp.where(some, size, 1.0)
            ratio = jnp.where(some, sin_h / safe, 0.5)
            cosine = 1.0 - 2.0 * (sin_h * sin_h)
            sine_ratio = 2.0 * (ratio * cos_h)
            along = 2.0 * (ratio * ratio) * (B[0] * S[0] + B[1] * S[1] + B[2] * S[2])
            cross = (
                B[1] * S[2] - B[2] * S[1],
                B[2] * S[0] - B[0] * S[2],
                B[0] * S[1] - B[1] * S[0],
            )
            for c in range(3):
                fields[c, rows, cols] = B[c]
                rot[c, rows, cols] = (cosine * S[c] + sine_ratio * cross[c]) + along * B[c]


def shards(vectors, classical_spins, coefficients):
    f32 = jnp.float32
    vmem = pl.BlockSpec(memory_space=pltpu.VMEM)
    dma = pltpu.SemaphoreType.DMA
    mid, edge = (NY, 2, 3, 8, 128), (2, NY, 3, 8, 128)
    parts = pl.pallas_call(
        field_kernel,
        name="fields",
        out_shape=(jax.ShapeDtypeStruct(mid, f32), jax.ShapeDtypeStruct(edge, f32)),
        in_specs=[
            pl.BlockSpec(memory_space=pltpu.SMEM),
            pl.BlockSpec(memory_space=pl.ANY),
            vmem,
        ],
        out_specs=(vmem, vmem),
        scratch_shapes=[
            pltpu.VMEM((4, VECS, ROWS, COLS), jnp.bfloat16),
            *[pltpu.VMEM((2, 24, 4, 8, COLS), f32)] * 4,
            pltpu.VMEM((24, 3, 8, COLS), f32),
            pltpu.VMEM((2, 8, COLS), f32),
            pltpu.VMEM((2, 8, COLS), f32),
            pltpu.VMEM((2, 3, BLOCKS, 64, 128), f32),
            pltpu.VMEM((2, 2, 3, NY, 64, 128), f32),
            pltpu.VMEM((2, 2, BLOCKS, 64, 128), f32),
            pltpu.VMEM((2, BLOCKS, 8, 128), f32),
            pltpu.VMEM((2, VEC, 2, 8, 128), f32),
            pltpu.VMEM(mid, f32), pltpu.VMEM(mid, f32),
            pltpu.VMEM(mid[1:], f32), pltpu.VMEM(mid[1:], f32),
            pltpu.VMEM(edge, f32), pltpu.VMEM(edge, f32),
            pltpu.VMEM((2, 3, 8, 128), f32), pltpu.VMEM((2, 3, 8, 128), f32),
            pltpu.VMEM((3 * ROWS, COLS), f32),
            pltpu.VMEM((VEC, 3, 8, 128), f32),
            dma, dma((2, 2)), dma((2, 2)), dma((2,)), dma((2,)), dma((2, VEC)), dma((2, VEC)),
            dma((3, NY)), dma((3, NY)), dma((3,)), dma((3,)), dma((3, NY)), dma((3, NY)),
            dma((VEC,)), dma((VEC,)),
        ],
        compiler_params=pltpu.CompilerParams(
            collective_id=0, has_side_effects=True, vmem_limit_bytes=60 << 20
        ),
    )(coefficients, vectors, classical_spins)
    out = jax.ShapeDtypeStruct((3, ROWS, COLS), f32)
    rotated, fields = pl.pallas_call(
        rotate_kernel,
        name="rotate",
        out_shape=(out, out),
        in_specs=[vmem, vmem, vmem],
        out_specs=(vmem, vmem),
    )(*parts, classical_spins)
    return rotated, fields


def solution(mesh):
    placed = (P(None, "vec", "lat", None), P(None, "lat", None), P())
    return jax.shard_map(
        shards,
        mesh=mesh,
        in_specs=placed,
        out_specs=(P(None, "lat", None), P(None, "lat", None)),
        check_vma=False,
    )
```

time: 46.3 us -> 39.6 us (0.86)
  Pallas kernels: 45.5 us -> 38.7 us
    pallas_call x1, Pallas kernels: 43.4 us -> 36.5 us  [shards(): pl.pallas_call(field_kernel, name='fields', out_shape=(jax.ShapeDtypeStru...]
where the time goes in v2:
time: 39.6 us; the launch traced here: 39.4 us
  Pallas kernels  38.7 us (98%)
  between operations  0.64 us (2%)
    pallas_call x1, Pallas kernels, shards(): pl.pallas_call(field_kernel, name='fields', out_shape=(jax.ShapeDtypeStru...  36.5 us
    pallas_call x1, Pallas kernels, shards(): pl.pallas_call(rotate_kernel, name='rotate', out_shape=(out, out), in_spe...  2.27 us

profile of v2, /device:TPU:0, one launch (start us, length us, event | category | flops | bytes accessed | tf_op | source)
XLA Modules:
  0.0 39.4 jit_solution(10122457976247252244)
XLA Ops:
  0.6 36.5 %fields.1 = (f32[4,2,3,8,128]{4,3,2,1,0:T(8,128)}, f32[2,4,3,8,128]{4,3,2,1,0:T(8,128)}) custom-call(f32[5]{0:T(128)} %coef.1, bf16[4,16,16,1024]{3,2,1,0:T(8,128)(2,1)} %x_hbm.1, f32[3,16,1024]{2,1,0:T(8,128)} %s_ref.1), custom_call_target="tpu_custom_call" | custom-call | tf_op jit(solution)/shard_map/fields/pallas_call | solution.py:537
  37.1 2.3 %rotate.1 = (f32[3,16,1024]{2,1,0:T(8,128)}, f32[3,16,1024]{2,1,0:T(8,128)}) custom-call(f32[4,2,3,8,128]{4,3,2,1,0:T(8,128)} %get-tuple-element.4.mid_ref, f32[2,4,3,8,128]{4,3,2,1,0:T(8,128)} %get-tuple-element.5.edge_ref, f32[3,16,1024]{2,1,0:T(8,128)} %s_ref.1), custom_call_target="tpu_custom_call" | custom-call | tf_op jit(solution)/shard_map/rotate/pallas_call | solution.py:573

commit v3 on v2

--- a/solution.py
+++ b/solution.py
@@ -63,10 +63,10 @@
 
 
 def field_kernel(
-    coef, x_hbm, s_vmem, out_mid, out_edge,
-    xv, R, W3, W2, W1, SB, SHs, SHr, DM, DE, E, PBs, PBr,
-    FM, RM, QM, XM, FE, RE, QE, XE, SP, RB,
-    xsem, hs, hr, ss, sr, ps, pr, ys_s, ys_r, xs_s, xs_r, yg_s, yg_r, bs_s, bs_r,
+    coef, x_hbm, s_hbm, out_mid, out_edge,
+    xv, s_vmem, R, W3, W2, W1, SB, SHs, SHr, DM, DE, E, PBs, PBr,
+    FM, RM, QM, XM, FE, RE, QE, XE, SP, GX,
+    xsem, ssem, hs, hr, ss, sr, ps, pr, ys_s, ys_r, xs_s, xs_r, yg_s, yg_r, bs_s, bs_r,
 ):
     lat, vec = lax.axis_index("lat"), lax.axis_index("vec")
     prev, nxt = lax.rem(lat + LAT - 1, LAT), lax.rem(lat + 1, LAT)
@@ -77,6 +77,8 @@
     def y_peer(d):
         return base + lax.rem(y + d, NY)
 
+    load_spins = pltpu.make_async_copy(s_hbm, s_vmem, ssem)
+    load_spins.start()
     load = pltpu.make_async_copy(x_hbm, xv, xsem)
     load.start()
 
@@ -95,21 +97,6 @@
     a4 = c4 * (8.0 * h * h * h * h)
 
     by_deal = deal()
-    for q in range(4):
-        cols = slice(q * 256, (q + 1) * 256)
-        SP[:, cols] = permuted(s_vmem[:, :, cols].reshape(3 * ROWS, 256), by_deal)
-    for c in range(3):
-        for k in range(2):
-            q, at = 2 * c + k, c * ROWS + k
-            SHs[0, q : q + 1, :] = SP[at : at + 1, :]
-            SHs[1, q : q + 1, :] = SP[at + 14 : at + 15, :]
-    for s in range(2):
-        SHs[s, 6:8, :] = jnp.zeros((2, COLS), jnp.float32)
-    zero = jnp.zeros((8, COLS), jnp.float32)
-    for row in range(ROWS):
-        for c in range(3):
-            at = c * ROWS + row
-            SB[PAD + row, c] = jnp.broadcast_to(2.0 * SP[at : at + 1, :], (8, COLS))
 
     def swap(order):
         n = 16 * len(order)
@@ -135,28 +122,44 @@
                         lo = at * 16 + g * 8
                         R[g, PAD + row, c, :, cols] = got[lo : lo + 8]
 
+    def spin_copy(s):
+        return pltpu.make_async_remote_copy(
+            SHs.at[s], SHr.at[1 - s], ss.at[s], sr.at[1 - s],
+            device_id={"lat": (prev, nxt)[s]}, device_id_type=MESH,
+        )
+
+    def halo_copy(s, g):
+        src, dst = ((4, 20), (18, 2))[s]
+        return pltpu.make_async_remote_copy(
+            R.at[g, pl.ds(src, 2)], R.at[g, pl.ds(dst, 2)], hs.at[s, g], hr.at[1 - s, g],
+            device_id={"lat": (prev, nxt)[s]}, device_id_type=MESH,
+        )
+
+    load_spins.wait()
+    for c in range(3):
+        for k in range(2):
+            q = 2 * c + k
+            SHs[0, q : q + 1, :] = s_vmem[c, k : k + 1, :]
+            SHs[1, q : q + 1, :] = s_vmem[c, 14 + k : 15 + k, :]
+    for s in range(2):
+        SHs[s, 6:8, :] = jnp.zeros((2, COLS), jnp.float32)
     load.wait()
     spread((0, 1, 14, 15))
     pl.semaphore_wait(barrier, 2 + 4)
-
-    def spin_copy(s):
-        return pltpu.make_async_remote_copy(
-            SHs.at[s], SHr.at[1 - s], ss.at[s], sr.at[1 - s],
-            device_id={"lat": (prev, nxt)[s]}, device_id_type=MESH,
-        )
-
-    def halo_copy(s, g):
-        src, dst = ((4, 20), (18, 2))[s]
-        return pltpu.make_async_remote_copy(
-            R.at[g, pl.ds(src, 2)], R.at[g, pl.ds(dst, 2)], hs.at[s, g], hr.at[1 - s, g],
-            device_id={"lat": (prev, nxt)[s]}, device_id_type=MESH,
-        )
-
     for s in range(2):
         spin_copy(s).start()
     for g in range(2):
         for s in range(2):
             halo_copy(s, g).start()
+
+    for q in range(4):
+        cols = slice(q * 256, (q + 1) * 256)
+        SP[:, cols] = permuted(s_vmem[:, :, cols].reshape(3 * ROWS, 256), by_deal)
+    zero = jnp.zeros((8, COLS), jnp.float32)
+    for row in range(ROWS):
+        for c in range(3):
+            at = c * ROWS + row
+            SB[PAD + row, c] = jnp.broadcast_to(2.0 * SP[at : at + 1, :], (8, COLS))
 
     spread(tuple(range(2, 14)))
     for c in range(3):
@@ -195,7 +198,7 @@
         return res
 
     def steps(groups, start, count, body):
-        each = STEPS_EACH // len(groups)
+        each = 2
 
         @pl.loop(0, count // each)
         def _(i):
@@ -274,20 +277,25 @@
         for d in range(1, NY):
             y_scatter(grp, d).start()
 
-    def exchange(grp):
+    def partial_sum(grp):
         for d in range(1, NY):
             y_scatter(grp, d).wait_recv()
         got, mine = refs(grp, RM, RE), refs(grp, FM, FE)
-        total = (mine[y] + got[1]) + (got[2] + got[3])
-        into = refs(grp, QM, QE)
+        return (mine[y] + got[1]) + (got[2] + got[3])
+
+    def edge_partial_sum(s, which, into):
+        total = partial_sum(s)
+        for d in range(NY):
+            push_copy(s, which, d).wait_recv()
+        extra = placed(s)
+        for c in range(3):
+            into[c] = total[c] + extra[c]
+
+    def exchange(grp):
         if grp is None:
-            into[...] = total
+            QM[...] = partial_sum(grp)
         else:
-            for d in range(NY):
-                chip_push(d).wait_recv()
-            extra = placed(grp, NY)
-            for c in range(3):
-                into[c] = total[c] + extra[c]
+            edge_partial_sum(grp, 0, QE.at[grp])
         x_exchange(grp).start()
 
     def gather(grp):
@@ -318,12 +326,17 @@
     scatter(None)
 
     for s in range(2):
-        spin_copy(s).wait()
-    for s in range(2):
-        for c in range(3):
-            for k in range(2):
-                q = 2 * c + k
-                SB[(2, 20)[s] + k, c] = jnp.broadcast_to(2.0 * SHr[s, q : q + 1, :], (8, COLS))
+        spin_copy(s).wait_recv()
+    for q in range(4):
+        cols = slice(q * 256, (q + 1) * 256)
+        got = 2.0 * permuted(SHr[:, :, cols].reshape(16, 256), by_deal)
+        for s in range(2):
+            for c in range(3):
+                for k in range(2):
+                    at = 8 * s + 2 * c + k
+                    SB[(2, 20)[s] + k, c, :, cols] = jnp.broadcast_to(
+                        got[at : at + 1], (8, 256)
+                    )
 
     def push(s, g):
         far, near = 2 + 11 * s + PAD, PAD - 1 + 17 * s
@@ -361,35 +374,27 @@
     def beyond(s):
         return lax.rem(lat + LAT - 1 + 2 * s, LAT)
 
-    def chip_push(d):
+    def push_copy(s, which, d):
         to = y_peer(d)
         return pltpu.make_async_remote_copy(
-            PBs.at[chip_side, pl.ds(2 * (to - base), 2)], PBr.at[1 - chip_side, d],
-            ps.at[0, d], pr.at[0, d],
-            device_id={"lat": beyond(chip_side), "vec": to}, device_id_type=MESH,
-        )
-
-    def link_push(d):
-        to = lax.rem(vec + d, VEC)
-        return pltpu.make_async_remote_copy(
-            PBs.at[link_side, pl.ds(2 * lax.rem(to, NY), 2)], PBr.at[1 - link_side, d],
-            ps.at[1, d], pr.at[1, d],
-            device_id={"lat": beyond(link_side), "vec": to}, device_id_type=MESH,
-        )
-
-    def link_scatter(d):
-        to = lax.rem(vec + d, VEC)
-        return pltpu.make_async_remote_copy(
-            FE.at[link_side, lax.rem(to, NY)], RB.at[d], bs_s.at[d], bs_r.at[d],
+            PBs.at[s, pl.ds(2 * (to - base), 2)], PBr.at[1 - s, d],
+            ps.at[which, d], pr.at[which, d],
+            device_id={"lat": beyond(s), "vec": to}, device_id_type=MESH,
+        )
+
+    def spread_sum(half, d):
+        to = lax.rem(base + NY * half, VEC) + lax.rem(y + d, NY)
+        return pltpu.make_async_remote_copy(
+            GX.at[0, y], GX.at[half, y], bs_s.at[half, d], bs_r.at[half, d],
             device_id={"vec": to}, device_id_type=MESH,
         )
 
+    others = [(0, 1), (0, 2), (0, 3), (1, 0), (1, 1), (1, 2), (1, 3)]
+
     sub = lax.broadcasted_iota(jnp.int32, (8, 128), 0)
 
-    def placed(s, count):
-        got = PBr[s, 0]
-        for d in range(1, count):
-            got = got + PBr[s, d]
+    def placed(s):
+        got = (PBr[s, 0] + PBr[s, 1]) + (PBr[s, 2] + PBr[s, 3])
         res = []
         for c in range(3):
             total = jnp.zeros((8, 128), jnp.float32)
@@ -420,12 +425,6 @@
     for g in range(2):
         wait_halo(s, g)
     wedge(s, (0, 1))
-    exchange(None)
-    for g in range(2):
-        push(s, g)
-    fold_push(s)
-    for d in range(NY):
-        chip_push(d).start()
     fold_edge(s)
     scatter(s)
 
@@ -433,47 +432,44 @@
     wait_halo(s, 0)
     push(s, 0)
     wedge(s, (0,))
-    gather(None)
-    exchange(chip_side)
+    exchange(None)
+    for g in range(2):
+        push(chip_side, g)
+    fold_push(chip_side)
+    for d in range(NY):
+        push_copy(chip_side, 0, d).start()
     wait_halo(s, 1)
     push(s, 1)
     fold_push(s)
-    for d in range(VEC):
-        link_push(d).start()
+    for d in range(NY):
+        push_copy(s, 1, d).start()
     wedge(s, (1,))
     fold_edge(s)
-    for d in range(1, VEC):
-        link_scatter(d).start()
+    scatter(s)
+    exchange(chip_side)
+    gather(None)
+    edge_partial_sum(s, 1, GX.at[0, y])
+    for half, d in others:
+        spread_sum(half, d).start()
     gather(chip_side)
-    for d in range(1, VEC):
-        link_scatter(d).wait_recv()
-    for d in range(VEC):
-        link_push(d).wait_recv()
-    extra = placed(s, VEC)
-    for c in range(3):
-        total = FE[s, y, c] + extra[c]
-        for d in range(1, VEC):
-            total = total + RB[d, c]
-        out_edge[s, y, c] = total
-    for d in range(1, NY):
-        y_gather(s, d).start()
 
     for s in range(2):
+        spin_copy(s).wait_send()
         for g in range(2):
             halo_copy(s, g).wait_send()
     for d in range(NY):
-        chip_push(d).wait_send()
-    for d in range(VEC):
-        link_push(d).wait_send()
-    for d in range(1, VEC):
-        link_scatter(d).wait_send()
+        push_copy(chip_side, 0, d).wait_send()
+        push_copy(link_side, 1, d).wait_send()
+    for d in range(1, NY):
+        y_scatter(link_side, d).wait_send()
     for grp in (None, chip_side):
         x_exchange(grp).wait_send()
         for d in range(1, NY):
             y_scatter(grp, d).wait_send()
             y_gather(grp, d).wait()
-    for d in range(1, NY):
-        y_gather(link_side, d).wait()
+    for half, d in others:
+        spread_sum(half, d).wait()
+    out_edge[link_side] = GX[0] + GX[1]
 
 
 def rotate_kernel(mid_ref, edge_ref, s_ref, rot, fields):
@@ -541,11 +537,12 @@
         in_specs=[
             pl.BlockSpec(memory_space=pltpu.SMEM),
             pl.BlockSpec(memory_space=pl.ANY),
-            vmem,
+            pl.BlockSpec(memory_space=pl.ANY),
         ],
         out_specs=(vmem, vmem),
         scratch_shapes=[
             pltpu.VMEM((4, VECS, ROWS, COLS), jnp.bfloat16),
+            pltpu.VMEM((3, ROWS, COLS), f32),
             *[pltpu.VMEM((2, 24, 4, 8, COLS), f32)] * 4,
             pltpu.VMEM((24, 3, 8, COLS), f32),
             pltpu.VMEM((2, 8, COLS), f32),
@@ -554,16 +551,17 @@
             pltpu.VMEM((2, 2, 3, NY, 64, 128), f32),
             pltpu.VMEM((2, 2, BLOCKS, 64, 128), f32),
             pltpu.VMEM((2, BLOCKS, 8, 128), f32),
-            pltpu.VMEM((2, VEC, 2, 8, 128), f32),
+            pltpu.VMEM((2, NY, 2, 8, 128), f32),
             pltpu.VMEM(mid, f32), pltpu.VMEM(mid, f32),
             pltpu.VMEM(mid[1:], f32), pltpu.VMEM(mid[1:], f32),
             pltpu.VMEM(edge, f32), pltpu.VMEM(edge, f32),
             pltpu.VMEM((2, 3, 8, 128), f32), pltpu.VMEM((2, 3, 8, 128), f32),
             pltpu.VMEM((3 * ROWS, COLS), f32),
-            pltpu.VMEM((VEC, 3, 8, 128), f32),
-            dma, dma((2, 2)), dma((2, 2)), dma((2,)), dma((2,)), dma((2, VEC)), dma((2, VEC)),
+            pltpu.VMEM(edge, f32),
+            dma, dma, dma((2, 2)), dma((2, 2)), dma((2,)), dma((2,)),
+            dma((2, NY)), dma((2, NY)),
             dma((3, NY)), dma((3, NY)), dma((3,)), dma((3,)), dma((3, NY)), dma((3, NY)),
-            dma((VEC,)), dma((VEC,)),
+            dma((2, NY)), dma((2, NY)),
         ],
         compiler_params=pltpu.CompilerParams(
             collective_id=0, has_side_effects=True, vmem_limit_bytes=60 << 20

time: 39.6 us -> 37.9 us (0.957)
  Pallas kernels: 38.7 us -> 37.1 us
    pallas_call x1, Pallas kernels: 36.5 us -> 34.8 us  [shards(): pl.pallas_call(field_kernel, name='fields', out_shape=(jax.ShapeDtypeStru...]
where the time goes in v3:
time: 37.9 us; the launch traced here: 37.7 us
  Pallas kernels  37.1 us (98%)
  between operations  0.64 us (2%)
    pallas_call x1, Pallas kernels, shards(): pl.pallas_call(field_kernel, name='fields', out_shape=(jax.ShapeDtypeStru...  34.8 us
    pallas_call x1, Pallas kernels, shards(): pl.pallas_call(rotate_kernel, name='rotate', out_shape=(out, out), in_spe...  2.27 us

profile of v3, /device:TPU:0, one launch (start us, length us, event | category | flops | bytes accessed | tf_op | source)
XLA Modules:
  0.0 37.7 jit_solution(5834050358812518831)
XLA Ops:
  0.6 34.8 %fields.1 = (f32[4,2,3,8,128]{4,3,2,1,0:T(8,128)}, f32[2,4,3,8,128]{4,3,2,1,0:T(8,128)}) custom-call(f32[5]{0:T(128)} %coef.1, bf16[4,16,16,1024]{3,2,1,0:T(8,128)(2,1)} %x_hbm.1, f32[3,16,1024]{2,1,0:T(8,128)} %s_ref.1), custom_call_target="tpu_custom_call" | custom-call | tf_op jit(solution)/shard_map/fields/pallas_call | solution.py:533
  35.5 2.3 %rotate.1 = (f32[3,16,1024]{2,1,0:T(8,128)}, f32[3,16,1024]{2,1,0:T(8,128)}) custom-call(f32[4,2,3,8,128]{4,3,2,1,0:T(8,128)} %get-tuple-element.4.mid_ref, f32[2,4,3,8,128]{4,3,2,1,0:T(8,128)} %get-tuple-element.5.edge_ref, f32[3,16,1024]{2,1,0:T(8,128)} %s_ref.1), custom_call_target="tpu_custom_call" | custom-call | tf_op jit(solution)/shard_map/rotate/pallas_call | solution.py:571
